TPU v7x, 32 devices: a whole 2x2x4 slice. The times are simulated.
32 devices in a mesh: energy: 16 (over z, y, x), slab: 2 (over core).
Axes of the slice: x: 2, y: 2, z: 4, core: 2. Of those that a mesh axis runs over, the one named last changes fastest.
Arguments:
- green0: bfloat16 [16, 2, 2, 384, 384], P('energy', 'slab'), may hold values from -6 to 6
- coupling: bfloat16 [2, 3, 384, 384], P('slab'), may hold values from -0.09375 to 0.09375
Outputs:
- green: bfloat16 [16, 2, 2, 384, 384], P('energy', 'slab')
All inputs are finite; a program needn't handle non-finite values.
Results may differ from a plain program's by a relative error of at most 0.012.
Values may be sent and summed in bfloat16 or wider, within the bound.
No kernel may reach another device: no remote copies, remote signals or barrier semaphores. Data moves between devices by JAX's collectives and lax.ppermute only.
A program may use at most 64 MiB of HBM per device.

v0:
```python
import functools

import jax
import jax.numpy as jnp
from jax import lax
from jax.experimental import pallas as pl
from jax.experimental.pallas import tpu as pltpu
from jax.sharding import PartitionSpec as P

OFFSET = 7
ITERS = 2
VMEM_LIMIT = 12 << 20
ROW, LAYER = 2, 4


def passed_along(value, axis, steps):
    count = lax.axis_size(axis)
    first, last = (max(0, -steps), min(count, count - steps))
    return lax.ppermute(value, axis, [(source, source + steps) for source in range(first, last)])


def with_halo(block, sides, width):
    for axis, dim in sides:
        count = lax.axis_size(axis)
        forward = [(i, i + 1) for i in range(count - 1)]
        backward = [(target, source) for source, target in forward]
        low = lax.ppermute(
            lax.slice_in_dim(block, block.shape[dim] - width, None, axis=dim), axis, forward
        )
        high = lax.ppermute(lax.slice_in_dim(block, 0, width, axis=dim), axis, backward)
        block = jnp.concatenate([low, block, high], axis=dim)
    return block


def dyson(green0, coupling, summed):
    count = green0.shape[1]
    size = green0.shape[-1]
    sigma = jnp.zeros(green0.shape, jnp.float32)
    for index in range(3):
        part = summed[:, index : index + count]
        weights = coupling[:, index]
        left = jnp.einsum(
            "sij,escjk->escik", weights, part, preferred_element_type=jnp.float32
        ).astype(jnp.bfloat16)
        sigma = sigma + jnp.einsum(
            "escij,skj->escik", left, weights, preferred_element_type=jnp.float32
        )
    sigma = sigma.astype(jnp.bfloat16)
    green_re = green0[:, :, 0]
    green_im = green0[:, :, 1]
    form = "esij,esjk->esik"
    prod_re = jnp.einsum(
        form, green_re, sigma[:, :, 0], preferred_element_type=jnp.float32
    ) - jnp.einsum(form, green_im, sigma[:, :, 1], preferred_element_type=jnp.float32)
    prod_im = jnp.einsum(
        form, green_re, sigma[:, :, 1], preferred_element_type=jnp.float32
    ) + jnp.einsum(form, green_im, sigma[:, :, 0], preferred_element_type=jnp.float32)
    prod_re = prod_re.astype(jnp.bfloat16)
    prod_im = prod_im.astype(jnp.bfloat16)
    trans = "esij,eskj->esik"
    out_re = jnp.einsum(trans, prod_re, green_re, preferred_element_type=jnp.float32) - jnp.einsum(
        trans, prod_im, green_im, preferred_element_type=jnp.float32
    )
    out_im = jnp.einsum(trans, prod_re, green_im, preferred_element_type=jnp.float32) + jnp.einsum(
        trans, prod_im, green_re, preferred_element_type=jnp.float32
    )
    result = green0.astype(jnp.float32) + jnp.stack([out_re, out_im], axis=2) / size
    return result.astype(jnp.bfloat16)


def plain(green0, coupling):
    green = green0
    for _ in range(ITERS):
        lower = passed_along(green, "energy", OFFSET)
        upper = passed_along(green, "energy", -OFFSET)
        own_sum = (lower.astype(jnp.float32) + upper.astype(jnp.float32)).astype(jnp.bfloat16)
        summed = with_halo(own_sum, (("slab", 1),), 1)
        green = dyson(green0, coupling, summed)
    return green


def links(source, target):
    passed, at = [], source
    for step, size in ((LAYER, None), (1, ROW), (ROW, LAYER)):
        here, there = ((e // step if size is None else e % size // step) for e in (at, target))
        for _ in range(abs(there - here)):
            to = at + (step if there > here else -step)
            passed.append((at, to))
            at = to
    return passed


def planned(energies):
    chains = [list(range(first, energies, OFFSET)) for first in range(min(OFFSET, energies))]
    threes = [chain for chain in chains if len(chain) == 3]
    twos = [chain for chain in chains if len(chain) == 2]
    if len(threes) != 2 or len(threes) + len(twos) != len(chains):
        return None
    (low0, mid0, high0), (low1, mid1, high1) = threes
    inward = [(low0, mid0), (low1, mid1), (high0, mid0), (high1, mid1)]
    plan = {
        "first": [],
        "other": [],
        "second": [],
        "inward_low": inward[:2],
        "inward_high": inward[2:],
        "back_low": [(mid0, low0), (mid1, low1)],
        "back_high": [(mid0, high0), (mid1, high1)],
    }
    busy = {link for flow in inward for link in links(*flow)}
    taken = set()
    direct, late, relays = [], [], []
    for source, target in [flow for a, b in twos for flow in ((a, b), (b, a))]:
        passed = set(links(source, target))
        relay = target - target % LAYER + source % LAYER
        if passed & taken or any(abs(a - b) == LAYER for a, b in passed & busy):
            plan["second"].append((source, target))
            late.append((source, target))
        elif passed & busy:
            plan["first"].append((source, relay))
            plan["second"].append((relay, target))
            relays.append((relay, target))
            taken |= set(links(source, relay))
        else:
            direct.append((source, target))
            taken |= passed
    relayed = {relay for relay, _ in relays}
    plan["first"] += [flow for flow in direct if flow[1] not in relayed]
    plan["other"] += [flow for flow in direct if flow[1] in relayed]
    for flows in plan.values():
        sources, targets = zip(*flows)
        if len(set(sources)) < len(flows) or len(set(targets)) < len(flows):
            return None
    plan["lows"], plan["mids"], plan["highs"] = ([a, b] for a, b in zip(*threes))
    plan["direct"] = [target for _, target in direct if target in relayed]
    plan["early"] = [target for _, target in direct if target not in relayed]
    plan["relayed"] = [relay for relay, _ in relays]
    plan["late"] = [source for source, _ in late]
    plan["second_pairs"] = [target for _, target in late + relays]
    return plan


def dot(left, right):
    return jnp.dot(left, right, preferred_element_type=jnp.float32)


def dot_t(left, right):
    return lax.dot_general(
        left, right, (((1,), (1,)), ((), ())), preferred_element_type=jnp.float32
    )


def among(members):
    energy = lax.axis_index("energy")
    return functools.reduce(jnp.logical_or, [energy == member for member in members])


def here(members, core):
    return jnp.logical_and(among(members), lax.axis_index("slab") == core)


def far_weight(weights):
    return weights[2 - 2 * lax.axis_index("slab")]


def self_energy(mine, other, weights):
    size = mine.shape[-1]
    own, far = weights[1], far_weight(weights)
    near = dot(own, jnp.concatenate([mine[0], mine[1]], axis=1)).astype(jnp.bfloat16)
    cross = dot(far, jnp.concatenate([other[0], other[1]], axis=1)).astype(jnp.bfloat16)
    left = jnp.concatenate(
        [
            jnp.concatenate([near[:, :size], cross[:, :size]], axis=1),
            jnp.concatenate([near[:, size:], cross[:, size:]], axis=1),
        ],
        axis=0,
    )
    return dot_t(left, jnp.concatenate([own, far], axis=1)).astype(jnp.bfloat16)


def around(re, im, block_re, block_im):
    square = jnp.concatenate(
        [
            jnp.concatenate([block_re, block_im], axis=1),
            jnp.concatenate([-block_im, block_re], axis=1),
        ],
        axis=0,
    )
    product = dot(jnp.concatenate([re, im], axis=1), square).astype(jnp.bfloat16)
    turned = jnp.concatenate(
        [jnp.concatenate([re, -im], axis=1), jnp.concatenate([im, re], axis=1)], axis=0
    )
    return dot_t(product, turned)


def onto(green, added):
    size = added.shape[0]
    return [
        green[part].astype(jnp.float32) + added[:, part * size : (part + 1) * size] / size
        for part in range(2)
    ]


def stepped(green, sigma):
    return onto(green, around(green[0], green[1], sigma[0], sigma[1]))


def put(out, parts):
    for part, value in enumerate(parts):
        out[part] = value.astype(out.dtype)


def added(one, two):
    return (one.astype(jnp.float32) + two.astype(jnp.float32)).astype(one.dtype)


def load_kernel(own, weights, own_out, weights_out, sems):
    copies = [
        pltpu.make_async_copy(own, own_out, sems.at[0]),
        pltpu.make_async_copy(weights, weights_out, sems.at[1]),
    ]
    for copy in copies:
        copy.start()
    for copy in copies:
        copy.wait()


def sigma_kernel(plan, own, beside, weights, out):
    size = own.shape[-1]

    @pl.when(jnp.logical_not(among(plan["lows"] + plan["highs"])))
    def _():
        sigma = self_energy(own, beside, weights)
        out[0] = sigma[:size]
        out[1] = sigma[size:]


def sum_kernel(plan, low, high, out, core):
    @pl.when(here(plan["mids"], core))
    def _():
        out[...] = added(low[...], high[...])


def turn_kernel(plan, own, weights, near, far):
    size = own.shape[-1]
    both = jnp.concatenate([weights[1], far_weight(weights)], axis=1)
    for part in range(2):
        turn = dot(own[part], both).astype(jnp.bfloat16)
        near[part] = turn[:, :size]
        far[part] = turn[:, size:]


def early_kernel(plan, near_turn, far_turn, both, across, out):
    @pl.when(here(plan["mids"], 0))
    def _():
        out[...] = around(near_turn[0], near_turn[1], both[0], both[1])

    @pl.when(here(plan["mids"], 1))
    def _():
        out[...] = around(far_turn[0], far_turn[1], across[0], across[1])


def second_kernel(plan, own, turn, near, both, first, send):
    @pl.when(here(plan["mids"], 1))
    def _():
        put(send, onto(own, near[...] + around(turn[0], turn[1], both[0], both[1])))

    for members, source in ((plan["relayed"], first), (plan["late"], own)):

        @pl.when(among(members))
        def _():
            send[...] = source[...]


def third_kernel(plan, own, turn, near, across, send):
    @pl.when(here(plan["mids"], 0))
    def _():
        put(send, onto(own, near[...] + around(turn[0], turn[1], across[0], across[1])))


def middle_kernel(plan, low0, high0, low1, high1, sigma, out):
    for core, blocks in enumerate(((low0, high0), (low1, high1))):

        @pl.when(here(plan["mids"], core))
        def _():
            steps = [stepped(block, sigma) for block in blocks]
            for part in range(2):
                out[part] = added(*(step[part].astype(out.dtype) for step in steps))


def neighbour_kernel(plan, first, other, second, low0, high0, low1, high1, middle, sigma, out):
    for members, source in (
        (plan["early"], first),
        (plan["direct"], other),
        (plan["second_pairs"], second),
    ):

        @pl.when(among(members))
        def _():
            put(out, stepped(source, sigma))

    ends = [
        (core, back[side], plan[members])
        for core, back in enumerate(((low0, high0), (low1, high1)))
        for side, members in enumerate(("lows", "highs"))
    ]
    for core, source, members in ends:

        @pl.when(here(members, core))
        def _():
            out[...] = source[...]

    @pl.when(among(plan["mids"]))
    def _():
        out[...] = middle[...]


def close_kernel(plan, turn, green, out):
    out[...] = around(turn[0], turn[1], green[0], green[1])


def last_kernel(plan, own, turn, near, across, out):
    put(out, onto(own, near[...] + around(turn[0], turn[1], across[0], across[1])))


LIMITS = pltpu.CompilerParams(vmem_limit_bytes=VMEM_LIMIT)
IN_VMEM = pl.BlockSpec(memory_space=pltpu.VMEM)
IN_HBM = pl.BlockSpec(memory_space=pltpu.HBM)


def like(block, space=jax.ShapeDtypeStruct):
    return space(block.shape, block.dtype)


def call(kernel, plan, *blocks, out=None, **options):
    return pl.pallas_call(
        functools.partial(kernel, plan, **options),
        out_shape=out or like(blocks[0]),
        in_specs=[IN_VMEM] * len(blocks),
        out_specs=[IN_VMEM] * len(out) if isinstance(out, list) else IN_VMEM,
        compiler_params=LIMITS,
    )(*blocks)


def loaded(own, weights):
    return pl.pallas_call(
        load_kernel,
        out_shape=[like(own), like(weights)],
        in_specs=[IN_HBM] * 2,
        out_specs=[IN_VMEM] * 2,
        scratch_shapes=[pltpu.SemaphoreType.DMA((2,))],
        compiler_params=LIMITS,
        name="load_kernel",
    )(own, weights)


def chained(plan, green0, coupling):
    slabs = lax.axis_size("slab")
    size = green0.shape[-1]
    wide = jax.ShapeDtypeStruct((size, 2 * size), jnp.float32)

    def sent(value, flows, cores=range(slabs)):
        pairs = [(a * slabs + s, b * slabs + s) for a, b in plan[flows] for s in cores]
        return lax.ppermute(value, ("energy", "slab"), pairs)

    def swapped(value):
        flows = [(s, slabs - 1 - s) for s in range(slabs)]
        return lax.ppermute(value, "slab", flows)

    def inward(value, core):
        return [sent(value, "inward_" + side, [core]) for side in SIDES]

    def back(value, core):
        return [sent(value, "back_" + side, [core]) for side in SIDES]

    given = green0[0, 0]
    far = pltpu.with_memory_space_constraint(given, pltpu.HBM)
    far_weights = pltpu.with_memory_space_constraint(coupling[0], pltpu.HBM)
    in0 = inward(given, 0)
    first, other = sent(given, "first"), sent(given, "other")
    own, weights = loaded(far, far_weights)
    in1 = inward(own, 1)
    sigma = call(sigma_kernel, plan, own, swapped(own), weights)
    near_turn, far_turn = call(turn_kernel, plan, own, weights, out=[like(own)] * 2)
    both = call(sum_kernel, plan, *in0, core=0)
    across = swapped(both)
    near = call(early_kernel, plan, near_turn, far_turn, both, across, out=wide)
    both = call(sum_kernel, plan, *in1, core=1)
    across = swapped(both)
    send = call(second_kernel, plan, own, near_turn, near, both, first)
    back1 = back(send, 1)
    second = sent(send, "second")
    send = call(third_kernel, plan, own, far_turn, near, across)
    back0 = back(send, 0)
    middle = call(middle_kernel, plan, *in0, *in1, sigma)
    green = call(neighbour_kernel, plan, first, other, second, *back0, *back1, middle, sigma)
    across = swapped(green)
    near = call(close_kernel, plan, near_turn, green, out=wide)
    out = call(last_kernel, plan, own, far_turn, near, across)
    return out[None, None]


SIDES = ("low", "high")


def solution(mesh):
    plan = planned(mesh.shape["energy"]) if mesh.shape["slab"] == 2 else None
    local = functools.partial(chained, plan) if plan else plain
    placed = (P("energy", "slab", None, None, None), P("slab", None, None, None))
    return jax.shard_map(
        local,
        mesh=mesh,
        in_specs=placed,
        out_specs=P("energy", "slab", None, None, None),
        check_vma=False,
    )
```

profile of v0, /device:TPU:0, one launch (start us, length us, event | category | flops | bytes accessed | tf_op | source)
XLA Modules:
  0.0 51.2 jit_solution(3232960443211564271)
XLA Ops:
  0.0 0.7 %collective-permute-start.3 = (bf16[2,384,384]{2,1,0:T(8,128)(2,1)}, bf16[2,384,384]{2,1,0:T(8,128)(2,1)S(1)}, u32[]{:S(2)}, u32[]{:S(2)}) collective-permute-start(bf16[2,384,384]{2,1,0:T(8,128)(2,1)} %bitcast.4), channel_id=1, source_target_pairs={{28,14},{30,16}} | collective-permute-start | bytes 1769480 | tf_op jit(solution)/shard_map/ppermute | solution.py:364
  0.7 7.5 %collective-permute-start.2 = (bf16[2,384,384]{2,1,0:T(8,128)(2,1)}, bf16[2,384,384]{2,1,0:T(8,128)(2,1)S(1)}, u32[]{:S(2)}, u32[]{:S(2)}) collective-permute-start(bf16[2,384,384]{2,1,0:T(8,128)(2,1)} %bitcast.5), channel_id=1, source_target_pairs={{0,14},{2,16}} | collective-permute-start | bytes 1769480 | tf_op jit(solution)/shard_map/ppermute | solution.py:364
  8.2 1.4 %load_kernel.1 = (bf16[2,384,384]{2,1,0:T(8,128)(2,1)S(1)}, bf16[3,384,384]{2,1,0:T(8,128)(2,1)S(1)}) custom-call(bf16[2,384,384]{2,1,0:T(8,128)(2,1)} %bitcast.6, bf16[3,384,384]{2,1,0:T(8,128)(2,1)} %bitcast.3), custom_call_target="tpu_custom_call" | custom-call | tf_op jit(solution)/shard_map/load_kernel/pallas_call | solution.py:346
  9.5 0.0 copy-start
  9.6 0.8 %collective-permute-start.6 = (bf16[2,384,384]{2,1,0:T(8,128)(2,1)S(1)}, bf16[2,384,384]{2,1,0:T(8,128)(2,1)S(1)}, u32[]{:S(2)}, u32[]{:S(2)}) collective-permute-start(bf16[2,384,384]{2,1,0:T(8,128)(2,1)S(1)} %get-tuple-element.9.own), channel_id=1, source_target_pairs={{29,15},{31,17}} | collective-permute-start | bytes 1769480 | tf_op jit(solution)/shard_map/ppermute | solution.py:364
  10.4 0.7 %collective-permute-start.5 = (bf16[2,384,384]{2,1,0:T(8,128)(2,1)S(1)}, bf16[2,384,384]{2,1,0:T(8,128)(2,1)S(1)}, u32[]{:S(2)}, u32[]{:S(2)}) collective-permute-start(bf16[2,384,384]{2,1,0:T(8,128)(2,1)S(1)} %get-tuple-element.9.own), channel_id=1, source_target_pairs={{1,15},{3,17}} | collective-permute-start | bytes 1769480 | tf_op jit(solution)/shard_map/ppermute | solution.py:364
  11.1 0.0 collective-permute-done.3.high.high0
  11.1 9.5 %collective-permute-done.2.low.low0 = bf16[2,384,384]{2,1,0:T(8,128)(2,1)S(1)} collective-permute-done((bf16[2,384,384]{2,1,0:T(8,128)(2,1)}, bf16[2,384,384]{2,1,0:T(8,128)(2,1)S(1)}, u32[]{:S(2)}, u32[]{:S(2)}) %collective-permute-start.2) | collective-permute-done | bytes 589856 | tf_op jit(solution)/shard_map/ppermute | solution.py:364
  20.6 0.0 collective-permute-start.4
  20.6 0.0 copy-done
  20.6 0.7 %collective-permute-start = (bf16[2,384,384]{2,1,0:T(8,128)(2,1)S(1)}, bf16[2,384,384]{2,1,0:T(8,128)(2,1)S(1)}, u32[]{:S(2)}, u32[]{:S(2)}) collective-permute-start(bf16[2,384,384]{2,1,0:T(8,128)(2,1)S(1)} %bitcast.7), channel_id=1, source_target_pairs={{6,22},{7,23},{24,8},{25,9},{4,18},{5,19},{18,4},{19,5}} | collective-permute-start | bytes 1769480 | tf_op jit(solution)/shard_map/ppermute | solution.py:364
  21.3 0.0 collective-permute-done.6.high.high1
  21.3 0.0 collective-permute-done.5.low.low1
  21.3 0.8 %collective-permute-start.8 = (bf16[2,384,384]{2,1,0:T(8,128)(2,1)S(1)}, bf16[2,384,384]{2,1,0:T(8,128)(2,1)S(1)}, u32[]{:S(2)}, u32[]{:S(2)}) collective-permute-start(bf16[2,384,384]{2,1,0:T(8,128)(2,1)S(1)} %shard_map.31.both), channel_id=1, source_target_pairs={{0,1},{1,0},{2,3},{3,2},{4,5},{5,4},{6,7},{7,6},{8,9},{9,8},{10,11... | collective-permute-start | bytes 1769480 | tf_op jit(solution)/shard_map/ppermute | solution.py:368
  22.2 0.7 %collective-permute-start.1 = (bf16[2,384,384]{2,1,0:T(8,128)(2,1)S(1)}, bf16[2,384,384]{2,1,0:T(8,128)(2,1)S(1)}, u32[]{:S(2)}, u32[]{:S(2)}) collective-permute-start(bf16[2,384,384]{2,1,0:T(8,128)(2,1)S(1)} %bitcast.8), channel_id=1, source_target_pairs={{8,22},{9,23},{22,8},{23,9}} | collective-permute-start | bytes 1769480 | tf_op jit(solution)/shard_map/ppermute | solution.py:364
  22.9 0.1 collective-permute-start.13
  22.9 0.8 %shard_map.28 = (bf16[2,384,384]{2,1,0:T(8,128)(2,1)S(1)}, bf16[2,384,384]{2,1,0:T(8,128)(2,1)S(1)}) custom-call(bf16[2,384,384]{2,1,0:T(8,128)(2,1)S(1)} %get-tuple-element.9.own, bf16[3,384,384]{2,1,0:T(8,128)(2,1)S(1)} %get-tuple-element.10.weights), custom_call_target="tpu_custom_call" | custom-call | tf_op jit(solution)/shard_map/pallas_call | solution.py:336
  23.7 0.0 collective-permute-done.4.across
  23.8 0.0 collective-permute-done.first
  23.8 0.7 %collective-permute-start.12 = (bf16[2,384,384]{2,1,0:T(8,128)(2,1)S(1)}, bf16[2,384,384]{2,1,0:T(8,128)(2,1)S(1)}, u32[]{:S(2)}, u32[]{:S(2)}) collective-permute-start(bf16[2,384,384]{2,1,0:T(8,128)(2,1)S(1)} %shard_map.32), channel_id=1, source_target_pairs={{15,29},{17,31}} | collective-permute-start | bytes 1769480 | tf_op jit(solution)/shard_map/ppermute | solution.py:364
  24.5 0.7 %collective-permute-start.11 = (bf16[2,384,384]{2,1,0:T(8,128)(2,1)S(1)}, bf16[2,384,384]{2,1,0:T(8,128)(2,1)S(1)}, u32[]{:S(2)}, u32[]{:S(2)}) collective-permute-start(bf16[2,384,384]{2,1,0:T(8,128)(2,1)S(1)} %shard_map.32), channel_id=1, source_target_pairs={{15,1},{17,3}} | collective-permute-start | bytes 1769480 | tf_op jit(solution)/shard_map/ppermute | solution.py:364
  25.2 0.0 collective-permute-done.8.across
  25.2 0.7 %collective-permute-start.7 = (bf16[2,384,384]{2,1,0:T(8,128)(2,1)S(1)}, bf16[2,384,384]{2,1,0:T(8,128)(2,1)S(1)}, u32[]{:S(2)}, u32[]{:S(2)}) collective-permute-start(bf16[2,384,384]{2,1,0:T(8,128)(2,1)S(1)} %shard_map.32), channel_id=1, source_target_pairs={{22,20},{23,21},{20,6},{21,7},{10,24},{11,25},{8,10},{9,11},{12,26... | collective-permute-start | bytes 1769480 | tf_op jit(solution)/shard_map/ppermute | solution.py:364
  26.0 0.0 collective-permute-done.1.other
  26.0 0.7 %collective-permute-start.10 = (bf16[2,384,384]{2,1,0:T(8,128)(2,1)S(1)}, bf16[2,384,384]{2,1,0:T(8,128)(2,1)S(1)}, u32[]{:S(2)}, u32[]{:S(2)}) collective-permute-start(bf16[2,384,384]{2,1,0:T(8,128)(2,1)S(1)} %shard_map.33), channel_id=1, source_target_pairs={{14,28},{16,30}} | collective-permute-start | bytes 1769480 | tf_op jit(solution)/shard_map/ppermute | solution.py:364
  26.7 0.0 collective-permute-done.13.beside
  26.7 1.3 %collective-permute-start.9 = (bf16[2,384,384]{2,1,0:T(8,128)(2,1)S(1)}, bf16[2,384,384]{2,1,0:T(8,128)(2,1)S(1)}, u32[]{:S(2)}, u32[]{:S(2)}) collective-permute-start(bf16[2,384,384]{2,1,0:T(8,128)(2,1)S(1)} %shard_map.33), channel_id=1, source_target_pairs={{14,0},{16,2}} | collective-permute-start | bytes 1769480 | tf_op jit(solution)/shard_map/ppermute | solution.py:364
  28.1 0.0 collective-permute-done.12.high1
  28.1 0.0 collective-permute-done.11.low1
  28.1 0.0 collective-permute-done.7.second
  28.1 0.0 collective-permute-done.10.high0
  28.1 19.0 %collective-permute-done.9.low0 = bf16[2,384,384]{2,1,0:T(8,128)(2,1)S(1)} collective-permute-done((bf16[2,384,384]{2,1,0:T(8,128)(2,1)S(1)}, bf16[2,384,384]{2,1,0:T(8,128)(2,1)S(1)}, u32[]{:S(2)}, u32[]{:S(2)}) %collective-permute-start.9) | collective-permute-done | bytes 589856 | tf_op jit(solution)/shard_map/ppermute | solution.py:364
  47.1 0.1 shard_map.36.green
  47.1 0.1 collective-permute-start.14
  47.2 1.2 %shard_map.37.near = f32[384,768]{1,0:T(8,128)S(1)} custom-call(bf16[2,384,384]{2,1,0:T(8,128)(2,1)S(1)} %get-tuple-element.12.near_turn.turn, bf16[2,384,384]{2,1,0:T(8,128)(2,1)S(1)} %shard_map.36.green), custom_call_target="tpu_custom_call" | custom-call | tf_op jit(solution)/shard_map/pallas_call | solution.py:336
  48.4 0.8 %collective-permute-done.14.across = bf16[2,384,384]{2,1,0:T(8,128)(2,1)S(1)} collective-permute-done((bf16[2,384,384]{2,1,0:T(8,128)(2,1)S(1)}, bf16[2,384,384]{2,1,0:T(8,128)(2,1)S(1)}, u32[]{:S(2)}, u32[]{:S(2)}) %collective-permute-start.14) | collective-permute-done | bytes 589856 | tf_op jit(solution)/shard_map/ppermute | solution.py:368
  49.2 2.0 %shard_map.38 = bf16[2,384,384]{2,1,0:T(8,128)(2,1)} custom-call(bf16[2,384,384]{2,1,0:T(8,128)(2,1)S(1)} %get-tuple-element.9.own, bf16[2,384,384]{2,1,0:T(8,128)(2,1)S(1)} %get-tuple-element.11.far_turn.turn, f32[384,768]{1,0:T(8,128)S(1)} %shard_map.37.near, bf16[2,384,384]{2,1,0:T(8,128)(2,1)S(1)} %collective-permute-done.14.across), custom_call_target="tpu_custom_call" | custom-call | tf_op jit(solution)/shard_map/pallas_call | solution.py:336
  (7 shorter events, 0.1 us)
Async XLA Ops:
  0.0 11.1 %collective-permute-start.3 = (bf16[2,384,384]{2,1,0:T(8,128)(2,1)}, bf16[2,384,384]{2,1,0:T(8,128)(2,1)S(1)}, u32[]{:S(2)}, u32[]{:S(2)}) collective-permute-start(bf16[2,384,384]{2,1,0:T(8,128)(2,1)} %bitcast.4), channel_id=1, source_target_pairs={{28,14},{30,16}} | collective-permute-start | bytes 1769480 | tf_op jit(solution)/shard_map/ppermute | solution.py:364
  0.7 19.9 %collective-permute-start.2 = (bf16[2,384,384]{2,1,0:T(8,128)(2,1)}, bf16[2,384,384]{2,1,0:T(8,128)(2,1)S(1)}, u32[]{:S(2)}, u32[]{:S(2)}) collective-permute-start(bf16[2,384,384]{2,1,0:T(8,128)(2,1)} %bitcast.5), channel_id=1, source_target_pairs={{0,14},{2,16}} | collective-permute-start | bytes 1769480 | tf_op jit(solution)/shard_map/ppermute | solution.py:364
  9.5 11.0 %copy-start = (bf16[1,1,2,384,384]{4,3,2,1,0:T(8,128)(2,1)S(1)}, bf16[1,1,2,384,384]{4,3,2,1,0:T(8,128)(2,1)}, u32[]{:S(2)}) copy-start(bf16[1,1,2,384,384]{4,3,2,1,0:T(8,128)(2,1)} %param.2) | copy-start | bytes 1769476
  9.6 11.7 %collective-permute-start.6 = (bf16[2,384,384]{2,1,0:T(8,128)(2,1)S(1)}, bf16[2,384,384]{2,1,0:T(8,128)(2,1)S(1)}, u32[]{:S(2)}, u32[]{:S(2)}) collective-permute-start(bf16[2,384,384]{2,1,0:T(8,128)(2,1)S(1)} %get-tuple-element.9.own), channel_id=1, source_target_pairs={{29,15},{31,17}} | collective-permute-start | bytes 1769480 | tf_op jit(solution)/shard_map/ppermute | solution.py:364
  10.4 10.9 %collective-permute-start.5 = (bf16[2,384,384]{2,1,0:T(8,128)(2,1)S(1)}, bf16[2,384,384]{2,1,0:T(8,128)(2,1)S(1)}, u32[]{:S(2)}, u32[]{:S(2)}) collective-permute-start(bf16[2,384,384]{2,1,0:T(8,128)(2,1)S(1)} %get-tuple-element.9.own), channel_id=1, source_target_pairs={{1,15},{3,17}} | collective-permute-start | bytes 1769480 | tf_op jit(solution)/shard_map/ppermute | solution.py:364
  20.6 3.2 %collective-permute-start.4 = (bf16[2,384,384]{2,1,0:T(8,128)(2,1)S(1)}, bf16[2,384,384]{2,1,0:T(8,128)(2,1)S(1)}, u32[]{:S(2)}, u32[]{:S(2)}) collective-permute-start(bf16[2,384,384]{2,1,0:T(8,128)(2,1)S(1)} %shard_map.29.both), channel_id=1, source_target_pairs={{0,1},{1,0},{2,3},{3,2},{4,5},{5,4},{6,7},{7,6},{8,9},{9,8},{10,11... | collective-permute-start | bytes 1769480 | tf_op jit(solution)/shard_map/ppermute | solution.py:368
  20.6 3.2 %collective-permute-start = (bf16[2,384,384]{2,1,0:T(8,128)(2,1)S(1)}, bf16[2,384,384]{2,1,0:T(8,128)(2,1)S(1)}, u32[]{:S(2)}, u32[]{:S(2)}) collective-permute-start(bf16[2,384,384]{2,1,0:T(8,128)(2,1)S(1)} %bitcast.7), channel_id=1, source_target_pairs={{6,22},{7,23},{24,8},{25,9},{4,18},{5,19},{18,4},{19,5}} | collective-permute-start | bytes 1769480 | tf_op jit(solution)/shard_map/ppermute | solution.py:364
  21.3 3.9 %collective-permute-start.8 = (bf16[2,384,384]{2,1,0:T(8,128)(2,1)S(1)}, bf16[2,384,384]{2,1,0:T(8,128)(2,1)S(1)}, u32[]{:S(2)}, u32[]{:S(2)}) collective-permute-start(bf16[2,384,384]{2,1,0:T(8,128)(2,1)S(1)} %shard_map.31.both), channel_id=1, source_target_pairs={{0,1},{1,0},{2,3},{3,2},{4,5},{5,4},{6,7},{7,6},{8,9},{9,8},{10,11... | collective-permute-start | bytes 1769480 | tf_op jit(solution)/shard_map/ppermute | solution.py:368
  22.2 3.8 %collective-permute-start.1 = (bf16[2,384,384]{2,1,0:T(8,128)(2,1)S(1)}, bf16[2,384,384]{2,1,0:T(8,128)(2,1)S(1)}, u32[]{:S(2)}, u32[]{:S(2)}) collective-permute-start(bf16[2,384,384]{2,1,0:T(8,128)(2,1)S(1)} %bitcast.8), channel_id=1, source_target_pairs={{8,22},{9,23},{22,8},{23,9}} | collective-permute-start | bytes 1769480 | tf_op jit(solution)/shard_map/ppermute | solution.py:364
  22.9 3.8 %collective-permute-start.13 = (bf16[2,384,384]{2,1,0:T(8,128)(2,1)S(1)}, bf16[2,384,384]{2,1,0:T(8,128)(2,1)S(1)}, u32[]{:S(2)}, u32[]{:S(2)}) collective-permute-start(bf16[2,384,384]{2,1,0:T(8,128)(2,1)S(1)} %get-tuple-element.9.own), channel_id=1, source_target_pairs={{0,1},{1,0},{2,3},{3,2},{4,5},{5,4},{6,7},{7,6},{8,9},{9,8},{10,11... | collective-permute-start | bytes 1769480 | tf_op jit(solution)/shard_map/ppermute | solution.py:368
  23.8 4.2 %collective-permute-start.12 = (bf16[2,384,384]{2,1,0:T(8,128)(2,1)S(1)}, bf16[2,384,384]{2,1,0:T(8,128)(2,1)S(1)}, u32[]{:S(2)}, u32[]{:S(2)}) collective-permute-start(bf16[2,384,384]{2,1,0:T(8,128)(2,1)S(1)} %shard_map.32), channel_id=1, source_target_pairs={{15,29},{17,31}} | collective-permute-start | bytes 1769480 | tf_op jit(solution)/shard_map/ppermute | solution.py:364
  24.5 3.5 %collective-permute-start.11 = (bf16[2,384,384]{2,1,0:T(8,128)(2,1)S(1)}, bf16[2,384,384]{2,1,0:T(8,128)(2,1)S(1)}, u32[]{:S(2)}, u32[]{:S(2)}) collective-permute-start(bf16[2,384,384]{2,1,0:T(8,128)(2,1)S(1)} %shard_map.32), channel_id=1, source_target_pairs={{15,1},{17,3}} | collective-permute-start | bytes 1769480 | tf_op jit(solution)/shard_map/ppermute | solution.py:364
  25.2 2.8 %collective-permute-start.7 = (bf16[2,384,384]{2,1,0:T(8,128)(2,1)S(1)}, bf16[2,384,384]{2,1,0:T(8,128)(2,1)S(1)}, u32[]{:S(2)}, u32[]{:S(2)}) collective-permute-start(bf16[2,384,384]{2,1,0:T(8,128)(2,1)S(1)} %shard_map.32), channel_id=1, source_target_pairs={{22,20},{23,21},{20,6},{21,7},{10,24},{11,25},{8,10},{9,11},{12,26... | collective-permute-start | bytes 1769480 | tf_op jit(solution)/shard_map/ppermute | solution.py:364
  26.0 2.1 %collective-permute-start.10 = (bf16[2,384,384]{2,1,0:T(8,128)(2,1)S(1)}, bf16[2,384,384]{2,1,0:T(8,128)(2,1)S(1)}, u32[]{:S(2)}, u32[]{:S(2)}) collective-permute-start(bf16[2,384,384]{2,1,0:T(8,128)(2,1)S(1)} %shard_map.33), channel_id=1, source_target_pairs={{14,28},{16,30}} | collective-permute-start | bytes 1769480 | tf_op jit(solution)/shard_map/ppermute | solution.py:364
  26.7 20.4 %collective-permute-start.9 = (bf16[2,384,384]{2,1,0:T(8,128)(2,1)S(1)}, bf16[2,384,384]{2,1,0:T(8,128)(2,1)S(1)}, u32[]{:S(2)}, u32[]{:S(2)}) collective-permute-start(bf16[2,384,384]{2,1,0:T(8,128)(2,1)S(1)} %shard_map.33), channel_id=1, source_target_pairs={{14,0},{16,2}} | collective-permute-start | bytes 1769480 | tf_op jit(solution)/shard_map/ppermute | solution.py:364
  47.1 2.1 %collective-permute-start.14 = (bf16[2,384,384]{2,1,0:T(8,128)(2,1)S(1)}, bf16[2,384,384]{2,1,0:T(8,128)(2,1)S(1)}, u32[]{:S(2)}, u32[]{:S(2)}) collective-permute-start(bf16[2,384,384]{2,1,0:T(8,128)(2,1)S(1)} %shard_map.36.green), channel_id=1, source_target_pairs={{0,1},{1,0},{2,3},{3,2},{4,5},{5,4},{6,7},{7,6},{8,9},{9,8},{10,11... | collective-permute-start | bytes 1769480 | tf_op jit(solution)/shard_map/ppermute | solution.py:368
where the time goes:
time: 51.5 us; the launch traced here: 51.2 us
  waiting for transfers between devices  29.2 us (57%)
  starting transfers between devices  16.1 us (31%)
  Pallas kernels  5.57 us (11%)
    ppermute x11, waiting for transfers between devices, sent(): return lax.ppermute(value, ('energy', 'slab'), pairs)  28.4 us
    ppermute x11, starting transfers between devices, sent(): return lax.ppermute(value, ('energy', 'slab'), pairs)  15.1 us
    pallas_call x11, Pallas kernels, call(): pl.pallas_call(functools.partial(kernel, plan, **options), out_shape=out...  4.21 us
    pallas_call x1, Pallas kernels, loaded(): pl.pallas_call(load_kernel, out_shape=[like(own), like(weights)], in_spec...  1.37 us
  transfers between devices with their start and end apart: 15, of which 3 were waited for; matrix products, arithmetic and copies ran while one was open for 0% of the time, Pallas kernels for 7%

commit v1 on v0

--- a/solution.py
+++ b/solution.py
@@ -178,7 +178,7 @@
     return dot_t(left, jnp.concatenate([own, far], axis=1)).astype(jnp.bfloat16)
 
 
-def around(re, im, block_re, block_im):
+def around_factors(re, im, block_re, block_im):
     square = jnp.concatenate(
         [
             jnp.concatenate([block_re, block_im], axis=1),
@@ -190,7 +190,11 @@
     turned = jnp.concatenate(
         [jnp.concatenate([re, -im], axis=1), jnp.concatenate([im, re], axis=1)], axis=0
     )
-    return dot_t(product, turned)
+    return product, turned
+
+
+def around(re, im, block_re, block_im):
+    return dot_t(*around_factors(re, im, block_re, block_im))
 
 
 def onto(green, added):
@@ -319,8 +323,26 @@
     out[...] = around(turn[0], turn[1], green[0], green[1])
 
 
-def last_kernel(plan, own, turn, near, across, out):
-    put(out, onto(own, near[...] + around(turn[0], turn[1], across[0], across[1])))
+def last_kernel(own, turn, near, across, out, held, sems):
+    size = own.shape[-1]
+    split = pl.cdiv(4 * size, 3)
+    product, turned = around_factors(turn[0], turn[1], across[0], across[1])
+    copies = [pltpu.make_async_copy(held.at[part], out.at[part], sems.at[part]) for part in (0, 1)]
+
+    def close(part, columns, added):
+        first = part * size + columns.start
+        green = own[part][:, columns].astype(jnp.float32)
+        total = near[:, first : first + added.shape[1]] + added
+        held[part, :, columns] = (green + total / size).astype(held.dtype)
+
+    added = dot_t(product, turned[:split])
+    close(0, slice(0, size), added[:, :size])
+    copies[0].start()
+    close(1, slice(0, split - size), added[:, size:])
+    close(1, slice(split - size, size), dot_t(product, turned[split:]))
+    copies[1].start()
+    for copy in copies:
+        copy.wait()
 
 
 LIMITS = pltpu.CompilerParams(vmem_limit_bytes=VMEM_LIMIT)
@@ -340,6 +362,18 @@
         out_specs=[IN_VMEM] * len(out) if isinstance(out, list) else IN_VMEM,
         compiler_params=LIMITS,
     )(*blocks)
+
+
+def ended(own, *blocks):
+    return pl.pallas_call(
+        last_kernel,
+        out_shape=like(own),
+        in_specs=[IN_VMEM] * (1 + len(blocks)),
+        out_specs=IN_HBM,
+        scratch_shapes=[like(own, pltpu.VMEM), pltpu.SemaphoreType.DMA((2,))],
+        compiler_params=LIMITS,
+        name="last_kernel",
+    )(own, *blocks)
 
 
 def loaded(own, weights):
@@ -396,7 +430,7 @@
     green = call(neighbour_kernel, plan, first, other, second, *back0, *back1, middle, sigma)
     across = swapped(green)
     near = call(close_kernel, plan, near_turn, green, out=wide)
-    out = call(last_kernel, plan, own, far_turn, near, across)
+    out = ended(own, far_turn, near, across)
     return out[None, None]
 
 

time: 51.5 us -> 51.6 us (level)
    pallas_call x11 -> x10, Pallas kernels: 4.21 us -> 2.18 us  [call(): pl.pallas_call(functools.partial(kernel, plan, **options), out_shape=out...]
    pallas_call x0 -> x1, Pallas kernels: none -> 1.94 us  [ended(): pl.pallas_call(last_kernel, out_shape=like(own), in_specs=[IN_VMEM] * (1...]
where the time goes in v1:
time: 51.6 us; the launch traced here: 51.3 us
  waiting for transfers between devices  29.2 us (57%)
  starting transfers between devices  16.1 us (31%)
  Pallas kernels  5.49 us (11%)
    ppermute x11, waiting for transfers between devices, sent(): return lax.ppermute(value, ('energy', 'slab'), pairs)  28.4 us
    ppermute x11, starting transfers between devices, sent(): return lax.ppermute(value, ('energy', 'slab'), pairs)  15.1 us
    pallas_call x10, Pallas kernels, call(): pl.pallas_call(functools.partial(kernel, plan, **options), out_shape=out...  2.18 us
    pallas_call x1, Pallas kernels, ended(): pl.pallas_call(last_kernel, out_shape=like(own), in_specs=[IN_VMEM] * (1...  1.94 us
    pallas_call x1, Pallas kernels, loaded(): pl.pallas_call(load_kernel, out_shape=[like(own), like(weights)], in_spec...  1.37 us
  transfers between devices with their start and end apart: 15, of which 3 were waited for; matrix products, arithmetic and copies ran while one was open for 0% of the time, Pallas kernels for 7%

profile of v1, /device:TPU:0, one launch (start us, length us, event | category | flops | bytes accessed | tf_op | source)
XLA Modules:
  0.0 51.3 jit_solution(11214947101310472626)
XLA Ops:
  0.0 0.7 %collective-permute-start.3 = (bf16[2,384,384]{2,1,0:T(8,128)(2,1)}, bf16[2,384,384]{2,1,0:T(8,128)(2,1)S(1)}, u32[]{:S(2)}, u32[]{:S(2)}) collective-permute-start(bf16[2,384,384]{2,1,0:T(8,128)(2,1)} %bitcast.4), channel_id=1, source_target_pairs={{28,14},{30,16}} | collective-permute-start | bytes 1769480 | tf_op jit(solution)/shard_map/ppermute | solution.py:398
  0.7 7.5 %collective-permute-start.2 = (bf16[2,384,384]{2,1,0:T(8,128)(2,1)}, bf16[2,384,384]{2,1,0:T(8,128)(2,1)S(1)}, u32[]{:S(2)}, u32[]{:S(2)}) collective-permute-start(bf16[2,384,384]{2,1,0:T(8,128)(2,1)} %bitcast.5), channel_id=1, source_target_pairs={{0,14},{2,16}} | collective-permute-start | bytes 1769480 | tf_op jit(solution)/shard_map/ppermute | solution.py:398
  8.2 1.4 %load_kernel.1 = (bf16[2,384,384]{2,1,0:T(8,128)(2,1)S(1)}, bf16[3,384,384]{2,1,0:T(8,128)(2,1)S(1)}) custom-call(bf16[2,384,384]{2,1,0:T(8,128)(2,1)} %bitcast.6, bf16[3,384,384]{2,1,0:T(8,128)(2,1)} %bitcast.3), custom_call_target="tpu_custom_call" | custom-call | tf_op jit(solution)/shard_map/load_kernel/pallas_call | solution.py:380
  9.5 0.0 copy-start
  9.6 0.8 %collective-permute-start.6 = (bf16[2,384,384]{2,1,0:T(8,128)(2,1)S(1)}, bf16[2,384,384]{2,1,0:T(8,128)(2,1)S(1)}, u32[]{:S(2)}, u32[]{:S(2)}) collective-permute-start(bf16[2,384,384]{2,1,0:T(8,128)(2,1)S(1)} %get-tuple-element.9.own), channel_id=1, source_target_pairs={{29,15},{31,17}} | collective-permute-start | bytes 1769480 | tf_op jit(solution)/shard_map/ppermute | solution.py:398
  10.4 0.7 %collective-permute-start.5 = (bf16[2,384,384]{2,1,0:T(8,128)(2,1)S(1)}, bf16[2,384,384]{2,1,0:T(8,128)(2,1)S(1)}, u32[]{:S(2)}, u32[]{:S(2)}) collective-permute-start(bf16[2,384,384]{2,1,0:T(8,128)(2,1)S(1)} %get-tuple-element.9.own), channel_id=1, source_target_pairs={{1,15},{3,17}} | collective-permute-start | bytes 1769480 | tf_op jit(solution)/shard_map/ppermute | solution.py:398
  11.1 0.0 collective-permute-done.3.high.high0
  11.1 9.5 %collective-permute-done.2.low.low0 = bf16[2,384,384]{2,1,0:T(8,128)(2,1)S(1)} collective-permute-done((bf16[2,384,384]{2,1,0:T(8,128)(2,1)}, bf16[2,384,384]{2,1,0:T(8,128)(2,1)S(1)}, u32[]{:S(2)}, u32[]{:S(2)}) %collective-permute-start.2) | collective-permute-done | bytes 589856 | tf_op jit(solution)/shard_map/ppermute | solution.py:398
  20.6 0.0 collective-permute-start.4
  20.6 0.0 copy-done
  20.6 0.7 %collective-permute-start = (bf16[2,384,384]{2,1,0:T(8,128)(2,1)S(1)}, bf16[2,384,384]{2,1,0:T(8,128)(2,1)S(1)}, u32[]{:S(2)}, u32[]{:S(2)}) collective-permute-start(bf16[2,384,384]{2,1,0:T(8,128)(2,1)S(1)} %bitcast.7), channel_id=1, source_target_pairs={{6,22},{7,23},{24,8},{25,9},{4,18},{5,19},{18,4},{19,5}} | collective-permute-start | bytes 1769480 | tf_op jit(solution)/shard_map/ppermute | solution.py:398
  21.3 0.0 collective-permute-done.6.high.high1
  21.3 0.0 collective-permute-done.5.low.low1
  21.3 0.8 %collective-permute-start.8 = (bf16[2,384,384]{2,1,0:T(8,128)(2,1)S(1)}, bf16[2,384,384]{2,1,0:T(8,128)(2,1)S(1)}, u32[]{:S(2)}, u32[]{:S(2)}) collective-permute-start(bf16[2,384,384]{2,1,0:T(8,128)(2,1)S(1)} %shard_map.31.both), channel_id=1, source_target_pairs={{0,1},{1,0},{2,3},{3,2},{4,5},{5,4},{6,7},{7,6},{8,9},{9,8},{10,11... | collective-permute-start | bytes 1769480 | tf_op jit(solution)/shard_map/ppermute | solution.py:402
  22.2 0.7 %collective-permute-start.1 = (bf16[2,384,384]{2,1,0:T(8,128)(2,1)S(1)}, bf16[2,384,384]{2,1,0:T(8,128)(2,1)S(1)}, u32[]{:S(2)}, u32[]{:S(2)}) collective-permute-start(bf16[2,384,384]{2,1,0:T(8,128)(2,1)S(1)} %bitcast.8), channel_id=1, source_target_pairs={{8,22},{9,23},{22,8},{23,9}} | collective-permute-start | bytes 1769480 | tf_op jit(solution)/shard_map/ppermute | solution.py:398
  22.9 0.1 collective-permute-start.13
  22.9 0.8 %shard_map.28 = (bf16[2,384,384]{2,1,0:T(8,128)(2,1)S(1)}, bf16[2,384,384]{2,1,0:T(8,128)(2,1)S(1)}) custom-call(bf16[2,384,384]{2,1,0:T(8,128)(2,1)S(1)} %get-tuple-element.9.own, bf16[3,384,384]{2,1,0:T(8,128)(2,1)S(1)} %get-tuple-element.10.weights), custom_call_target="tpu_custom_call" | custom-call | tf_op jit(solution)/shard_map/pallas_call | solution.py:358
  23.7 0.0 collective-permute-done.4.across
  23.8 0.0 collective-permute-done.first
  23.8 0.7 %collective-permute-start.12 = (bf16[2,384,384]{2,1,0:T(8,128)(2,1)S(1)}, bf16[2,384,384]{2,1,0:T(8,128)(2,1)S(1)}, u32[]{:S(2)}, u32[]{:S(2)}) collective-permute-start(bf16[2,384,384]{2,1,0:T(8,128)(2,1)S(1)} %shard_map.32), channel_id=1, source_target_pairs={{15,29},{17,31}} | collective-permute-start | bytes 1769480 | tf_op jit(solution)/shard_map/ppermute | solution.py:398
  24.5 0.7 %collective-permute-start.11 = (bf16[2,384,384]{2,1,0:T(8,128)(2,1)S(1)}, bf16[2,384,384]{2,1,0:T(8,128)(2,1)S(1)}, u32[]{:S(2)}, u32[]{:S(2)}) collective-permute-start(bf16[2,384,384]{2,1,0:T(8,128)(2,1)S(1)} %shard_map.32), channel_id=1, source_target_pairs={{15,1},{17,3}} | collective-permute-start | bytes 1769480 | tf_op jit(solution)/shard_map/ppermute | solution.py:398
  25.2 0.0 collective-permute-done.8.across
  25.2 0.7 %collective-permute-start.7 = (bf16[2,384,384]{2,1,0:T(8,128)(2,1)S(1)}, bf16[2,384,384]{2,1,0:T(8,128)(2,1)S(1)}, u32[]{:S(2)}, u32[]{:S(2)}) collective-permute-start(bf16[2,384,384]{2,1,0:T(8,128)(2,1)S(1)} %shard_map.32), channel_id=1, source_target_pairs={{22,20},{23,21},{20,6},{21,7},{10,24},{11,25},{8,10},{9,11},{12,26... | collective-permute-start | bytes 1769480 | tf_op jit(solution)/shard_map/ppermute | solution.py:398
  26.0 0.0 collective-permute-done.1.other
  26.0 0.7 %collective-permute-start.10 = (bf16[2,384,384]{2,1,0:T(8,128)(2,1)S(1)}, bf16[2,384,384]{2,1,0:T(8,128)(2,1)S(1)}, u32[]{:S(2)}, u32[]{:S(2)}) collective-permute-start(bf16[2,384,384]{2,1,0:T(8,128)(2,1)S(1)} %shard_map.33), channel_id=1, source_target_pairs={{14,28},{16,30}} | collective-permute-start | bytes 1769480 | tf_op jit(solution)/shard_map/ppermute | solution.py:398
  26.7 0.0 collective-permute-done.13.beside
  26.7 1.3 %collective-permute-start.9 = (bf16[2,384,384]{2,1,0:T(8,128)(2,1)S(1)}, bf16[2,384,384]{2,1,0:T(8,128)(2,1)S(1)}, u32[]{:S(2)}, u32[]{:S(2)}) collective-permute-start(bf16[2,384,384]{2,1,0:T(8,128)(2,1)S(1)} %shard_map.33), channel_id=1, source_target_pairs={{14,0},{16,2}} | collective-permute-start | bytes 1769480 | tf_op jit(solution)/shard_map/ppermute | solution.py:398
  28.1 0.0 collective-permute-done.12.high1
  28.1 0.0 collective-permute-done.11.low1
  28.1 0.0 collective-permute-done.7.second
  28.1 0.0 collective-permute-done.10.high0
  28.1 19.0 %collective-permute-done.9.low0 = bf16[2,384,384]{2,1,0:T(8,128)(2,1)S(1)} collective-permute-done((bf16[2,384,384]{2,1,0:T(8,128)(2,1)S(1)}, bf16[2,384,384]{2,1,0:T(8,128)(2,1)S(1)}, u32[]{:S(2)}, u32[]{:S(2)}) %collective-permute-start.9) | collective-permute-done | bytes 589856 | tf_op jit(solution)/shard_map/ppermute | solution.py:398
  47.1 0.1 shard_map.36.green
  47.1 0.1 collective-permute-start.14
  47.2 1.2 %shard_map.37.near = f32[384,768]{1,0:T(8,128)S(1)} custom-call(bf16[2,384,384]{2,1,0:T(8,128)(2,1)S(1)} %get-tuple-element.12.near_turn.turn, bf16[2,384,384]{2,1,0:T(8,128)(2,1)S(1)} %shard_map.36.green), custom_call_target="tpu_custom_call" | custom-call | tf_op jit(solution)/shard_map/pallas_call | solution.py:358
  48.4 0.8 %collective-permute-done.14.across = bf16[2,384,384]{2,1,0:T(8,128)(2,1)S(1)} collective-permute-done((bf16[2,384,384]{2,1,0:T(8,128)(2,1)S(1)}, bf16[2,384,384]{2,1,0:T(8,128)(2,1)S(1)}, u32[]{:S(2)}, u32[]{:S(2)}) %collective-permute-start.14) | collective-permute-done | bytes 589856 | tf_op jit(solution)/shard_map/ppermute | solution.py:402
  49.2 1.9 %last_kernel.1 = bf16[2,384,384]{2,1,0:T(8,128)(2,1)} custom-call(bf16[2,384,384]{2,1,0:T(8,128)(2,1)S(1)} %get-tuple-element.9.own, bf16[2,384,384]{2,1,0:T(8,128)(2,1)S(1)} %get-tuple-element.11.far_turn.turn, f32[384,768]{1,0:T(8,128)S(1)} %shard_map.37.near, bf16[2,384,384]{2,1,0:T(8,128)(2,1)S(1)} %collective-permute-done.14.across), custom_call_target="tpu_custom_call" | custom-call | tf_op jit(solution)/shard_map/last_kernel/pallas_call | solution.py:368
  (7 shorter events, 0.1 us)
Async XLA Ops:
  0.0 11.1 %collective-permute-start.3 = (bf16[2,384,384]{2,1,0:T(8,128)(2,1)}, bf16[2,384,384]{2,1,0:T(8,128)(2,1)S(1)}, u32[]{:S(2)}, u32[]{:S(2)}) collective-permute-start(bf16[2,384,384]{2,1,0:T(8,128)(2,1)} %bitcast.4), channel_id=1, source_target_pairs={{28,14},{30,16}} | collective-permute-start | bytes 1769480 | tf_op jit(solution)/shard_map/ppermute | solution.py:398
  0.7 19.9 %collective-permute-start.2 = (bf16[2,384,384]{2,1,0:T(8,128)(2,1)}, bf16[2,384,384]{2,1,0:T(8,128)(2,1)S(1)}, u32[]{:S(2)}, u32[]{:S(2)}) collective-permute-start(bf16[2,384,384]{2,1,0:T(8,128)(2,1)} %bitcast.5), channel_id=1, source_target_pairs={{0,14},{2,16}} | collective-permute-start | bytes 1769480 | tf_op jit(solution)/shard_map/ppermute | solution.py:398
  9.5 11.0 %copy-start = (bf16[1,1,2,384,384]{4,3,2,1,0:T(8,128)(2,1)S(1)}, bf16[1,1,2,384,384]{4,3,2,1,0:T(8,128)(2,1)}, u32[]{:S(2)}) copy-start(bf16[1,1,2,384,384]{4,3,2,1,0:T(8,128)(2,1)} %param.2) | copy-start | bytes 1769476
  9.6 11.7 %collective-permute-start.6 = (bf16[2,384,384]{2,1,0:T(8,128)(2,1)S(1)}, bf16[2,384,384]{2,1,0:T(8,128)(2,1)S(1)}, u32[]{:S(2)}, u32[]{:S(2)}) collective-permute-start(bf16[2,384,384]{2,1,0:T(8,128)(2,1)S(1)} %get-tuple-element.9.own), channel_id=1, source_target_pairs={{29,15},{31,17}} | collective-permute-start | bytes 1769480 | tf_op jit(solution)/shard_map/ppermute | solution.py:398
  10.4 10.9 %collective-permute-start.5 = (bf16[2,384,384]{2,1,0:T(8,128)(2,1)S(1)}, bf16[2,384,384]{2,1,0:T(8,128)(2,1)S(1)}, u32[]{:S(2)}, u32[]{:S(2)}) collective-permute-start(bf16[2,384,384]{2,1,0:T(8,128)(2,1)S(1)} %get-tuple-element.9.own), channel_id=1, source_target_pairs={{1,15},{3,17}} | collective-permute-start | bytes 1769480 | tf_op jit(solution)/shard_map/ppermute | solution.py:398
  20.6 3.2 %collective-permute-start.4 = (bf16[2,384,384]{2,1,0:T(8,128)(2,1)S(1)}, bf16[2,384,384]{2,1,0:T(8,128)(2,1)S(1)}, u32[]{:S(2)}, u32[]{:S(2)}) collective-permute-start(bf16[2,384,384]{2,1,0:T(8,128)(2,1)S(1)} %shard_map.29.both), channel_id=1, source_target_pairs={{0,1},{1,0},{2,3},{3,2},{4,5},{5,4},{6,7},{7,6},{8,9},{9,8},{10,11... | collective-permute-start | bytes 1769480 | tf_op jit(solution)/shard_map/ppermute | solution.py:402
  20.6 3.2 %collective-permute-start = (bf16[2,384,384]{2,1,0:T(8,128)(2,1)S(1)}, bf16[2,384,384]{2,1,0:T(8,128)(2,1)S(1)}, u32[]{:S(2)}, u32[]{:S(2)}) collective-permute-start(bf16[2,384,384]{2,1,0:T(8,128)(2,1)S(1)} %bitcast.7), channel_id=1, source_target_pairs={{6,22},{7,23},{24,8},{25,9},{4,18},{5,19},{18,4},{19,5}} | collective-permute-start | bytes 1769480 | tf_op jit(solution)/shard_map/ppermute | solution.py:398
  21.3 3.9 %collective-permute-start.8 = (bf16[2,384,384]{2,1,0:T(8,128)(2,1)S(1)}, bf16[2,384,384]{2,1,0:T(8,128)(2,1)S(1)}, u32[]{:S(2)}, u32[]{:S(2)}) collective-permute-start(bf16[2,384,384]{2,1,0:T(8,128)(2,1)S(1)} %shard_map.31.both), channel_id=1, source_target_pairs={{0,1},{1,0},{2,3},{3,2},{4,5},{5,4},{6,7},{7,6},{8,9},{9,8},{10,11... | collective-permute-start | bytes 1769480 | tf_op jit(solution)/shard_map/ppermute | solution.py:402
  22.2 3.8 %collective-permute-start.1 = (bf16[2,384,384]{2,1,0:T(8,128)(2,1)S(1)}, bf16[2,384,384]{2,1,0:T(8,128)(2,1)S(1)}, u32[]{:S(2)}, u32[]{:S(2)}) collective-permute-start(bf16[2,384,384]{2,1,0:T(8,128)(2,1)S(1)} %bitcast.8), channel_id=1, source_target_pairs={{8,22},{9,23},{22,8},{23,9}} | collective-permute-start | bytes 1769480 | tf_op jit(solution)/shard_map/ppermute | solution.py:398
  22.9 3.8 %collective-permute-start.13 = (bf16[2,384,384]{2,1,0:T(8,128)(2,1)S(1)}, bf16[2,384,384]{2,1,0:T(8,128)(2,1)S(1)}, u32[]{:S(2)}, u32[]{:S(2)}) collective-permute-start(bf16[2,384,384]{2,1,0:T(8,128)(2,1)S(1)} %get-tuple-element.9.own), channel_id=1, source_target_pairs={{0,1},{1,0},{2,3},{3,2},{4,5},{5,4},{6,7},{7,6},{8,9},{9,8},{10,11... | collective-permute-start | bytes 1769480 | tf_op jit(solution)/shard_map/ppermute | solution.py:402
  23.8 4.2 %collective-permute-start.12 = (bf16[2,384,384]{2,1,0:T(8,128)(2,1)S(1)}, bf16[2,384,384]{2,1,0:T(8,128)(2,1)S(1)}, u32[]{:S(2)}, u32[]{:S(2)}) collective-permute-start(bf16[2,384,384]{2,1,0:T(8,128)(2,1)S(1)} %shard_map.32), channel_id=1, source_target_pairs={{15,29},{17,31}} | collective-permute-start | bytes 1769480 | tf_op jit(solution)/shard_map/ppermute | solution.py:398
  24.5 3.5 %collective-permute-start.11 = (bf16[2,384,384]{2,1,0:T(8,128)(2,1)S(1)}, bf16[2,384,384]{2,1,0:T(8,128)(2,1)S(1)}, u32[]{:S(2)}, u32[]{:S(2)}) collective-permute-start(bf16[2,384,384]{2,1,0:T(8,128)(2,1)S(1)} %shard_map.32), channel_id=1, source_target_pairs={{15,1},{17,3}} | collective-permute-start | bytes 1769480 | tf_op jit(solution)/shard_map/ppermute | solution.py:398
  25.2 2.8 %collective-permute-start.7 = (bf16[2,384,384]{2,1,0:T(8,128)(2,1)S(1)}, bf16[2,384,384]{2,1,0:T(8,128)(2,1)S(1)}, u32[]{:S(2)}, u32[]{:S(2)}) collective-permute-start(bf16[2,384,384]{2,1,0:T(8,128)(2,1)S(1)} %shard_map.32), channel_id=1, source_target_pairs={{22,20},{23,21},{20,6},{21,7},{10,24},{11,25},{8,10},{9,11},{12,26... | collective-permute-start | bytes 1769480 | tf_op jit(solution)/shard_map/ppermute | solution.py:398
  26.0 2.1 %collective-permute-start.10 = (bf16[2,384,384]{2,1,0:T(8,128)(2,1)S(1)}, bf16[2,384,384]{2,1,0:T(8,128)(2,1)S(1)}, u32[]{:S(2)}, u32[]{:S(2)}) collective-permute-start(bf16[2,384,384]{2,1,0:T(8,128)(2,1)S(1)} %shard_map.33), channel_id=1, source_target_pairs={{14,28},{16,30}} | collective-permute-start | bytes 1769480 | tf_op jit(solution)/shard_map/ppermute | solution.py:398
  26.7 20.4 %collective-permute-start.9 = (bf16[2,384,384]{2,1,0:T(8,128)(2,1)S(1)}, bf16[2,384,384]{2,1,0:T(8,128)(2,1)S(1)}, u32[]{:S(2)}, u32[]{:S(2)}) collective-permute-start(bf16[2,384,384]{2,1,0:T(8,128)(2,1)S(1)} %shard_map.33), channel_id=1, source_target_pairs={{14,0},{16,2}} | collective-permute-start | bytes 1769480 | tf_op jit(solution)/shard_map/ppermute | solution.py:398
  47.1 2.1 %collective-permute-start.14 = (bf16[2,384,384]{2,1,0:T(8,128)(2,1)S(1)}, bf16[2,384,384]{2,1,0:T(8,128)(2,1)S(1)}, u32[]{:S(2)}, u32[]{:S(2)}) collective-permute-start(bf16[2,384,384]{2,1,0:T(8,128)(2,1)S(1)} %shard_map.36.green), channel_id=1, source_target_pairs={{0,1},{1,0},{2,3},{3,2},{4,5},{5,4},{6,7},{7,6},{8,9},{9,8},{10,11... | collective-permute-start | bytes 1769480 | tf_op jit(solution)/shard_map/ppermute | solution.py:402

commit v2 on v0

--- a/solution.py
+++ b/solution.py
@@ -178,19 +178,28 @@
     return dot_t(left, jnp.concatenate([own, far], axis=1)).astype(jnp.bfloat16)
 
 
-def around(re, im, block_re, block_im):
+def first_product(turn, block, first=0):
+    columns = slice(first, first + block.shape[1])
     square = jnp.concatenate(
         [
-            jnp.concatenate([block_re, block_im], axis=1),
-            jnp.concatenate([-block_im, block_re], axis=1),
+            jnp.concatenate([block[0], block[1]], axis=1),
+            jnp.concatenate([-block[1], block[0]], axis=1),
         ],
         axis=0,
     )
-    product = dot(jnp.concatenate([re, im], axis=1), square).astype(jnp.bfloat16)
+    return dot(jnp.concatenate([turn[0][:, columns], turn[1][:, columns]], axis=1), square)
+
+
+def second_product(product, turn):
+    re, im = turn[0], turn[1]
     turned = jnp.concatenate(
         [jnp.concatenate([re, -im], axis=1), jnp.concatenate([im, re], axis=1)], axis=0
     )
-    return dot_t(product, turned)
+    return dot_t(product.astype(jnp.bfloat16), turned)
+
+
+def around(turn, block):
+    return second_product(first_product(turn, block), turn)
 
 
 def onto(green, added):
@@ -202,7 +211,7 @@
 
 
 def stepped(green, sigma):
-    return onto(green, around(green[0], green[1], sigma[0], sigma[1]))
+    return onto(green, around(green, sigma))
 
 
 def put(out, parts):
@@ -253,17 +262,17 @@
 def early_kernel(plan, near_turn, far_turn, both, across, out):
     @pl.when(here(plan["mids"], 0))
     def _():
-        out[...] = around(near_turn[0], near_turn[1], both[0], both[1])
+        out[...] = around(near_turn, both)
 
     @pl.when(here(plan["mids"], 1))
     def _():
-        out[...] = around(far_turn[0], far_turn[1], across[0], across[1])
+        out[...] = around(far_turn, across)
 
 
 def second_kernel(plan, own, turn, near, both, first, send):
     @pl.when(here(plan["mids"], 1))
     def _():
-        put(send, onto(own, near[...] + around(turn[0], turn[1], both[0], both[1])))
+        put(send, onto(own, near[...] + around(turn, both)))
 
     for members, source in ((plan["relayed"], first), (plan["late"], own)):
 
@@ -272,10 +281,18 @@
             send[...] = source[...]
 
 
-def third_kernel(plan, own, turn, near, across, send):
+def put_cut(head, tail, parts):
+    cut = head.shape[1]
+    for part in range(2):
+        value = parts[part].astype(head.dtype)
+        head[part] = value[:cut]
+        tail[part] = value[cut:]
+
+
+def third_kernel(plan, own, turn, near, across, head, tail):
     @pl.when(here(plan["mids"], 0))
     def _():
-        put(send, onto(own, near[...] + around(turn[0], turn[1], across[0], across[1])))
+        put_cut(head, tail, onto(own, near[...] + around(turn, across)))
 
 
 def middle_kernel(plan, low0, high0, low1, high1, sigma, out):
@@ -288,7 +305,9 @@
                 out[part] = added(*(step[part].astype(out.dtype) for step in steps))
 
 
-def neighbour_kernel(plan, first, other, second, low0, high0, low1, high1, middle, sigma, out):
+def neighbour_kernel(
+    plan, first, other, second, low0, high0, low1, high1, middle, sigma, head, tail
+):
     for members, source in (
         (plan["early"], first),
         (plan["direct"], other),
@@ -297,30 +316,51 @@
 
         @pl.when(among(members))
         def _():
-            put(out, stepped(source, sigma))
-
-    ends = [
-        (core, back[side], plan[members])
-        for core, back in enumerate(((low0, high0), (low1, high1)))
-        for side, members in enumerate(("lows", "highs"))
-    ]
-    for core, source, members in ends:
-
-        @pl.when(here(members, core))
+            put_cut(head, tail, stepped(source, sigma))
+
+    for members, source in ((plan["lows"], low0), (plan["highs"], high0)):
+
+        @pl.when(here(members, 0))
+        def _():
+            head[...] = source[...]
+
+    for members, source in ((plan["lows"], low1), (plan["highs"], high1)):
+
+        @pl.when(here(members, 1))
+        def _():
+            put_cut(head, tail, source)
+
+    @pl.when(among(plan["mids"]))
+    def _():
+        put_cut(head, tail, middle)
+
+
+def tail_kernel(plan, made, low, high, out):
+    is_low, is_high = here(plan["lows"], 0), here(plan["highs"], 0)
+
+    @pl.when(jnp.logical_not(jnp.logical_or(is_low, is_high)))
+    def _():
+        out[...] = made[...]
+
+    for is_here, source in ((is_low, low), (is_high, high)):
+
+        @pl.when(is_here)
         def _():
             out[...] = source[...]
 
-    @pl.when(among(plan["mids"]))
-    def _():
-        out[...] = middle[...]
-
-
-def close_kernel(plan, turn, green, out):
-    out[...] = around(turn[0], turn[1], green[0], green[1])
-
-
-def last_kernel(plan, own, turn, near, across, out):
-    put(out, onto(own, near[...] + around(turn[0], turn[1], across[0], across[1])))
+
+def head_kernel(plan, near_turn, far_turn, mine, across, near, far):
+    near[...] = first_product(near_turn, mine)
+    far[...] = first_product(far_turn, across)
+
+
+def close_kernel(plan, turn, product, tail, out, cut):
+    out[...] = second_product(product[...] + first_product(turn, tail, cut), turn)
+
+
+def last_kernel(plan, own, turn, near, product, tail, out, cut):
+    total = near[...] + second_product(product[...] + first_product(turn, tail, cut), turn)
+    put(out, onto(own, total))
 
 
 LIMITS = pltpu.CompilerParams(vmem_limit_bytes=VMEM_LIMIT)
@@ -358,6 +398,10 @@
     slabs = lax.axis_size("slab")
     size = green0.shape[-1]
     wide = jax.ShapeDtypeStruct((size, 2 * size), jnp.float32)
+    cut = size - size // 3
+    cut_shapes = [
+        jax.ShapeDtypeStruct((2, rows, size), green0.dtype) for rows in (cut, size - cut)
+    ]
 
     def sent(value, flows, cores=range(slabs)):
         pairs = [(a * slabs + s, b * slabs + s) for a, b in plan[flows] for s in cores]
@@ -390,13 +434,22 @@
     send = call(second_kernel, plan, own, near_turn, near, both, first)
     back1 = back(send, 1)
     second = sent(send, "second")
-    send = call(third_kernel, plan, own, far_turn, near, across)
-    back0 = back(send, 0)
+    head, tail = call(third_kernel, plan, own, far_turn, near, across, out=cut_shapes)
+    heads, tails = back(head, 0), back(tail, 0)
     middle = call(middle_kernel, plan, *in0, *in1, sigma)
-    green = call(neighbour_kernel, plan, first, other, second, *back0, *back1, middle, sigma)
-    across = swapped(green)
-    near = call(close_kernel, plan, near_turn, green, out=wide)
-    out = call(last_kernel, plan, own, far_turn, near, across)
+    head, tail = call(
+        neighbour_kernel, plan, first, other, second, *heads, *back1, middle, sigma, out=cut_shapes
+    )
+    across = swapped(head)
+    near, far_product = call(
+        head_kernel, plan, near_turn, far_turn, head, across, out=[wide, wide]
+    )
+    tail = call(tail_kernel, plan, tail, *tails)
+    across = swapped(tail)
+    near = call(close_kernel, plan, near_turn, near, tail, out=wide, cut=cut)
+    out = call(
+        last_kernel, plan, own, far_turn, near, far_product, across, out=like(own), cut=cut
+    )
     return out[None, None]
 
 

time: 51.5 us -> 58.3 us (1.13)
  waiting for transfers between devices: 29.2 us -> 33.8 us
  starting transfers between devices: 16.1 us -> 18.2 us
    ppermute x11 -> x13, waiting for transfers between devices: 28.4 us -> 33.8 us  [sent(): return lax.ppermute(value, ('energy', 'slab'), pairs)]
    ppermute x11 -> x13, starting transfers between devices: 15.1 us -> 17.1 us  [sent(): return lax.ppermute(value, ('energy', 'slab'), pairs)]
    ppermute x4 -> x5, waiting for transfers between devices: 0.79 us -> 0.01 us  [swapped(): return lax.ppermute(value, 'slab', flows)]
    pallas_call x11 -> x13, Pallas kernels: 4.21 us -> 4.41 us  [call(): pl.pallas_call(functools.partial(kernel, plan, **options), out_shape=out...]
  transfers between devices with their start and end apart: 15 -> 18, of which waited for: 3 -> 3; matrix products, arithmetic and copies ran while one was open for 0% -> 0% of each run, Pallas kernels for 7% -> 7%
where the time goes in v2:
time: 58.3 us; the launch traced here: 58 us
  waiting for transfers between devices  33.8 us (58%)
  starting transfers between devices  18.2 us (31%)
  Pallas kernels  5.77 us (10%)
    ppermute x13, waiting for transfers between devices, sent(): return lax.ppermute(value, ('energy', 'slab'), pairs)  33.8 us
    ppermute x13, starting transfers between devices, sent(): return lax.ppermute(value, ('energy', 'slab'), pairs)  17.1 us
    pallas_call x13, Pallas kernels, call(): pl.pallas_call(functools.partial(kernel, plan, **options), out_shape=out...  4.41 us
    pallas_call x1, Pallas kernels, loaded(): pl.pallas_call(load_kernel, out_shape=[like(own), like(weights)], in_spec...  1.37 us
  transfers between devices with their start and end apart: 18, of which 3 were waited for; matrix products, arithmetic and copies ran while one was open for 0% of the time, Pallas kernels for 7%

profile of v2, /device:TPU:0, one launch (start us, length us, event | category | flops | bytes accessed | tf_op | source)
XLA Modules:
  0.0 58.0 jit_solution(14672689551993804197)
XLA Ops:
  0.0 0.7 %collective-permute-start.3 = (bf16[2,384,384]{2,1,0:T(8,128)(2,1)}, bf16[2,384,384]{2,1,0:T(8,128)(2,1)S(1)}, u32[]{:S(2)}, u32[]{:S(2)}) collective-permute-start(bf16[2,384,384]{2,1,0:T(8,128)(2,1)} %bitcast.4), channel_id=1, source_target_pairs={{28,14},{30,16}} | collective-permute-start | bytes 1769480 | tf_op jit(solution)/shard_map/ppermute | solution.py:408
  0.7 7.5 %collective-permute-start.2 = (bf16[2,384,384]{2,1,0:T(8,128)(2,1)}, bf16[2,384,384]{2,1,0:T(8,128)(2,1)S(1)}, u32[]{:S(2)}, u32[]{:S(2)}) collective-permute-start(bf16[2,384,384]{2,1,0:T(8,128)(2,1)} %bitcast.5), channel_id=1, source_target_pairs={{0,14},{2,16}} | collective-permute-start | bytes 1769480 | tf_op jit(solution)/shard_map/ppermute | solution.py:408
  8.2 1.4 %load_kernel.1 = (bf16[2,384,384]{2,1,0:T(8,128)(2,1)S(1)}, bf16[3,384,384]{2,1,0:T(8,128)(2,1)S(1)}) custom-call(bf16[2,384,384]{2,1,0:T(8,128)(2,1)} %bitcast.6, bf16[3,384,384]{2,1,0:T(8,128)(2,1)} %bitcast.3), custom_call_target="tpu_custom_call" | custom-call | tf_op jit(solution)/shard_map/load_kernel/pallas_call | solution.py:386
  9.5 0.0 copy-start
  9.6 0.8 %collective-permute-start.6 = (bf16[2,384,384]{2,1,0:T(8,128)(2,1)S(1)}, bf16[2,384,384]{2,1,0:T(8,128)(2,1)S(1)}, u32[]{:S(2)}, u32[]{:S(2)}) collective-permute-start(bf16[2,384,384]{2,1,0:T(8,128)(2,1)S(1)} %get-tuple-element.15.own), channel_id=1, source_target_pairs={{29,15},{31,17}} | collective-permute-start | bytes 1769480 | tf_op jit(solution)/shard_map/ppermute | solution.py:408
  10.4 0.7 %collective-permute-start.5 = (bf16[2,384,384]{2,1,0:T(8,128)(2,1)S(1)}, bf16[2,384,384]{2,1,0:T(8,128)(2,1)S(1)}, u32[]{:S(2)}, u32[]{:S(2)}) collective-permute-start(bf16[2,384,384]{2,1,0:T(8,128)(2,1)S(1)} %get-tuple-element.15.own), channel_id=1, source_target_pairs={{1,15},{3,17}} | collective-permute-start | bytes 1769480 | tf_op jit(solution)/shard_map/ppermute | solution.py:408
  11.1 0.0 collective-permute-done.3.high.high0
  11.1 9.5 %collective-permute-done.2.low.low0 = bf16[2,384,384]{2,1,0:T(8,128)(2,1)S(1)} collective-permute-done((bf16[2,384,384]{2,1,0:T(8,128)(2,1)}, bf16[2,384,384]{2,1,0:T(8,128)(2,1)S(1)}, u32[]{:S(2)}, u32[]{:S(2)}) %collective-permute-start.2) | collective-permute-done | bytes 589856 | tf_op jit(solution)/shard_map/ppermute | solution.py:408
  20.6 0.0 collective-permute-start.4
  20.6 0.0 copy-done
  20.6 0.7 %collective-permute-start = (bf16[2,384,384]{2,1,0:T(8,128)(2,1)S(1)}, bf16[2,384,384]{2,1,0:T(8,128)(2,1)S(1)}, u32[]{:S(2)}, u32[]{:S(2)}) collective-permute-start(bf16[2,384,384]{2,1,0:T(8,128)(2,1)S(1)} %bitcast.7), channel_id=1, source_target_pairs={{6,22},{7,23},{24,8},{25,9},{4,18},{5,19},{18,4},{19,5}} | collective-permute-start | bytes 1769480 | tf_op jit(solution)/shard_map/ppermute | solution.py:408
  21.3 0.0 collective-permute-done.6.high.high1
  21.3 0.0 collective-permute-done.5.low.low1
  21.3 0.8 %collective-permute-start.8 = (bf16[2,384,384]{2,1,0:T(8,128)(2,1)S(1)}, bf16[2,384,384]{2,1,0:T(8,128)(2,1)S(1)}, u32[]{:S(2)}, u32[]{:S(2)}) collective-permute-start(bf16[2,384,384]{2,1,0:T(8,128)(2,1)S(1)} %shard_map.31.both), channel_id=1, source_target_pairs={{0,1},{1,0},{2,3},{3,2},{4,5},{5,4},{6,7},{7,6},{8,9},{9,8},{10,11... | collective-permute-start | bytes 1769480 | tf_op jit(solution)/shard_map/ppermute | solution.py:412
  22.2 0.7 %collective-permute-start.1 = (bf16[2,384,384]{2,1,0:T(8,128)(2,1)S(1)}, bf16[2,384,384]{2,1,0:T(8,128)(2,1)S(1)}, u32[]{:S(2)}, u32[]{:S(2)}) collective-permute-start(bf16[2,384,384]{2,1,0:T(8,128)(2,1)S(1)} %bitcast.8), channel_id=1, source_target_pairs={{8,22},{9,23},{22,8},{23,9}} | collective-permute-start | bytes 1769480 | tf_op jit(solution)/shard_map/ppermute | solution.py:408
  22.9 0.1 collective-permute-start.13
  22.9 0.8 %shard_map.28 = (bf16[2,384,384]{2,1,0:T(8,128)(2,1)S(1)}, bf16[2,384,384]{2,1,0:T(8,128)(2,1)S(1)}) custom-call(bf16[2,384,384]{2,1,0:T(8,128)(2,1)S(1)} %get-tuple-element.15.own, bf16[3,384,384]{2,1,0:T(8,128)(2,1)S(1)} %get-tuple-element.16.weights), custom_call_target="tpu_custom_call" | custom-call | tf_op jit(solution)/shard_map/pallas_call | solution.py:376
  23.7 0.0 collective-permute-done.4.across
  23.8 0.0 collective-permute-done.first
  23.8 0.7 %collective-permute-start.12 = (bf16[2,384,384]{2,1,0:T(8,128)(2,1)S(1)}, bf16[2,384,384]{2,1,0:T(8,128)(2,1)S(1)}, u32[]{:S(2)}, u32[]{:S(2)}) collective-permute-start(bf16[2,384,384]{2,1,0:T(8,128)(2,1)S(1)} %shard_map.32), channel_id=1, source_target_pairs={{15,29},{17,31}} | collective-permute-start | bytes 1769480 | tf_op jit(solution)/shard_map/ppermute | solution.py:408
  24.5 0.7 %collective-permute-start.11 = (bf16[2,384,384]{2,1,0:T(8,128)(2,1)S(1)}, bf16[2,384,384]{2,1,0:T(8,128)(2,1)S(1)}, u32[]{:S(2)}, u32[]{:S(2)}) collective-permute-start(bf16[2,384,384]{2,1,0:T(8,128)(2,1)S(1)} %shard_map.32), channel_id=1, source_target_pairs={{15,1},{17,3}} | collective-permute-start | bytes 1769480 | tf_op jit(solution)/shard_map/ppermute | solution.py:408
  25.2 0.0 collective-permute-done.8.across
  25.2 0.7 %collective-permute-start.7 = (bf16[2,384,384]{2,1,0:T(8,128)(2,1)S(1)}, bf16[2,384,384]{2,1,0:T(8,128)(2,1)S(1)}, u32[]{:S(2)}, u32[]{:S(2)}) collective-permute-start(bf16[2,384,384]{2,1,0:T(8,128)(2,1)S(1)} %shard_map.32), channel_id=1, source_target_pairs={{22,20},{23,21},{20,6},{21,7},{10,24},{11,25},{8,10},{9,11},{12,26... | collective-permute-start | bytes 1769480 | tf_op jit(solution)/shard_map/ppermute | solution.py:408
  26.0 0.0 collective-permute-done.1.other
  26.0 0.7 %collective-permute-start.10 = (bf16[2,256,384]{2,1,0:T(8,128)(2,1)S(1)}, bf16[2,256,384]{2,1,0:T(8,128)(2,1)S(1)}, u32[]{:S(2)}, u32[]{:S(2)}) collective-permute-start(bf16[2,256,384]{2,1,0:T(8,128)(2,1)S(1)} %get-tuple-element.19), channel_id=1, source_target_pairs={{14,28},{16,30}} | collective-permute-start | bytes 1179656 | tf_op jit(solution)/shard_map/ppermute | solution.py:408
  26.7 0.0 collective-permute-done.13.beside
  26.7 1.3 %collective-permute-start.9 = (bf16[2,256,384]{2,1,0:T(8,128)(2,1)S(1)}, bf16[2,256,384]{2,1,0:T(8,128)(2,1)S(1)}, u32[]{:S(2)}, u32[]{:S(2)}) collective-permute-start(bf16[2,256,384]{2,1,0:T(8,128)(2,1)S(1)} %get-tuple-element.19), channel_id=1, source_target_pairs={{14,0},{16,2}} | collective-permute-start | bytes 1179656 | tf_op jit(solution)/shard_map/ppermute | solution.py:408
  28.1 0.0 collective-permute-done.10.high0
  28.1 0.7 %collective-permute-start.16 = (bf16[2,128,384]{2,1,0:T(8,128)(2,1)S(1)}, bf16[2,128,384]{2,1,0:T(8,128)(2,1)S(1)}, u32[]{:S(2)}, u32[]{:S(2)}) collective-permute-start(bf16[2,128,384]{2,1,0:T(8,128)(2,1)S(1)} %get-tuple-element.23), channel_id=1, source_target_pairs={{14,28},{16,30}} | collective-permute-start | bytes 589832 | tf_op jit(solution)/shard_map/ppermute | solution.py:408
  28.7 16.2 %collective-permute-done.9.low0 = bf16[2,256,384]{2,1,0:T(8,128)(2,1)S(1)} collective-permute-done((bf16[2,256,384]{2,1,0:T(8,128)(2,1)S(1)}, bf16[2,256,384]{2,1,0:T(8,128)(2,1)S(1)}, u32[]{:S(2)}, u32[]{:S(2)}) %collective-permute-start.9) | collective-permute-done | bytes 393248 | tf_op jit(solution)/shard_map/ppermute | solution.py:408
  45.0 0.0 collective-permute-done.12.high1
  45.0 0.0 collective-permute-done.11.low1
  45.0 0.0 collective-permute-done.7.second
  45.0 0.3 shard_map.36
  45.2 0.1 collective-permute-start.14
  45.3 1.3 %collective-permute-start.15 = (bf16[2,128,384]{2,1,0:T(8,128)(2,1)S(1)}, bf16[2,128,384]{2,1,0:T(8,128)(2,1)S(1)}, u32[]{:S(2)}, u32[]{:S(2)}) collective-permute-start(bf16[2,128,384]{2,1,0:T(8,128)(2,1)S(1)} %get-tuple-element.23), channel_id=1, source_target_pairs={{14,0},{16,2}} | collective-permute-start | bytes 589832 | tf_op jit(solution)/shard_map/ppermute | solution.py:408
  46.6 0.0 collective-permute-done.16.high
  46.6 8.1 %collective-permute-done.15.low = bf16[2,128,384]{2,1,0:T(8,128)(2,1)S(1)} collective-permute-done((bf16[2,128,384]{2,1,0:T(8,128)(2,1)S(1)}, bf16[2,128,384]{2,1,0:T(8,128)(2,1)S(1)}, u32[]{:S(2)}, u32[]{:S(2)}) %collective-permute-start.15) | collective-permute-done | bytes 196640 | tf_op jit(solution)/shard_map/ppermute | solution.py:408
  54.7 0.1 collective-permute-start.17
  54.8 0.0 collective-permute-done.14.across
  54.8 0.8 %shard_map.37 = (f32[384,768]{1,0:T(8,128)S(1)}, f32[384,768]{1,0:T(8,128)S(1)}) custom-call(bf16[2,384,384]{2,1,0:T(8,128)(2,1)S(1)} %get-tuple-element.18.near_turn.turn, bf16[2,384,384]{2,1,0:T(8,128)(2,1)S(1)} %get-tuple-element.17.far_turn.turn, bf16[2,256,384]{2,1,0:T(8,128)(2,1)S(1)} %get-tuple-element.20.mine, ...), custom_call_target="tpu_custom_call" | custom-call | tf_op jit(solution)/shard_map/pallas_call | solution.py:376
  55.6 0.8 %shard_map.39.near = f32[384,768]{1,0:T(8,128)S(1)} custom-call(bf16[2,384,384]{2,1,0:T(8,128)(2,1)S(1)} %get-tuple-element.18.near_turn.turn, f32[384,768]{1,0:T(8,128)S(1)} %get-tuple-element.21.product, bf16[2,128,384]{2,1,0:T(8,128)(2,1)S(1)} %shard_map.38.tail), custom_call_target="tpu_custom_call" | custom-call | tf_op jit(solution)/shard_map/pallas_call | solution.py:376
  56.4 0.0 collective-permute-done.17.tail
  56.4 1.6 %shard_map.40 = bf16[2,384,384]{2,1,0:T(8,128)(2,1)} custom-call(bf16[2,384,384]{2,1,0:T(8,128)(2,1)S(1)} %get-tuple-element.15.own, bf16[2,384,384]{2,1,0:T(8,128)(2,1)S(1)} %get-tuple-element.17.far_turn.turn, f32[384,768]{1,0:T(8,128)S(1)} %shard_map.39.near, f32[384,768]{1,0:T(8,128)S(1)} %get-tuple-element.24.product, ...), custom_call_target="tpu_custom_call" | custom-call | tf_op jit(solution)/shard_map/pallas_call | solution.py:376
  (8 shorter events, 0.1 us)
Async XLA Ops:
  0.0 11.1 %collective-permute-start.3 = (bf16[2,384,384]{2,1,0:T(8,128)(2,1)}, bf16[2,384,384]{2,1,0:T(8,128)(2,1)S(1)}, u32[]{:S(2)}, u32[]{:S(2)}) collective-permute-start(bf16[2,384,384]{2,1,0:T(8,128)(2,1)} %bitcast.4), channel_id=1, source_target_pairs={{28,14},{30,16}} | collective-permute-start | bytes 1769480 | tf_op jit(solution)/shard_map/ppermute | solution.py:408
  0.7 19.9 %collective-permute-start.2 = (bf16[2,384,384]{2,1,0:T(8,128)(2,1)}, bf16[2,384,384]{2,1,0:T(8,128)(2,1)S(1)}, u32[]{:S(2)}, u32[]{:S(2)}) collective-permute-start(bf16[2,384,384]{2,1,0:T(8,128)(2,1)} %bitcast.5), channel_id=1, source_target_pairs={{0,14},{2,16}} | collective-permute-start | bytes 1769480 | tf_op jit(solution)/shard_map/ppermute | solution.py:408
  9.5 11.0 %copy-start = (bf16[1,1,2,384,384]{4,3,2,1,0:T(8,128)(2,1)S(1)}, bf16[1,1,2,384,384]{4,3,2,1,0:T(8,128)(2,1)}, u32[]{:S(2)}) copy-start(bf16[1,1,2,384,384]{4,3,2,1,0:T(8,128)(2,1)} %param.2) | copy-start | bytes 1769476
  9.6 11.7 %collective-permute-start.6 = (bf16[2,384,384]{2,1,0:T(8,128)(2,1)S(1)}, bf16[2,384,384]{2,1,0:T(8,128)(2,1)S(1)}, u32[]{:S(2)}, u32[]{:S(2)}) collective-permute-start(bf16[2,384,384]{2,1,0:T(8,128)(2,1)S(1)} %get-tuple-element.15.own), channel_id=1, source_target_pairs={{29,15},{31,17}} | collective-permute-start | bytes 1769480 | tf_op jit(solution)/shard_map/ppermute | solution.py:408
  10.4 10.9 %collective-permute-start.5 = (bf16[2,384,384]{2,1,0:T(8,128)(2,1)S(1)}, bf16[2,384,384]{2,1,0:T(8,128)(2,1)S(1)}, u32[]{:S(2)}, u32[]{:S(2)}) collective-permute-start(bf16[2,384,384]{2,1,0:T(8,128)(2,1)S(1)} %get-tuple-element.15.own), channel_id=1, source_target_pairs={{1,15},{3,17}} | collective-permute-start | bytes 1769480 | tf_op jit(solution)/shard_map/ppermute | solution.py:408
  20.6 3.2 %collective-permute-start.4 = (bf16[2,384,384]{2,1,0:T(8,128)(2,1)S(1)}, bf16[2,384,384]{2,1,0:T(8,128)(2,1)S(1)}, u32[]{:S(2)}, u32[]{:S(2)}) collective-permute-start(bf16[2,384,384]{2,1,0:T(8,128)(2,1)S(1)} %shard_map.29.both), channel_id=1, source_target_pairs={{0,1},{1,0},{2,3},{3,2},{4,5},{5,4},{6,7},{7,6},{8,9},{9,8},{10,11... | collective-permute-start | bytes 1769480 | tf_op jit(solution)/shard_map/ppermute | solution.py:412
  20.6 3.2 %collective-permute-start = (bf16[2,384,384]{2,1,0:T(8,128)(2,1)S(1)}, bf16[2,384,384]{2,1,0:T(8,128)(2,1)S(1)}, u32[]{:S(2)}, u32[]{:S(2)}) collective-permute-start(bf16[2,384,384]{2,1,0:T(8,128)(2,1)S(1)} %bitcast.7), channel_id=1, source_target_pairs={{6,22},{7,23},{24,8},{25,9},{4,18},{5,19},{18,4},{19,5}} | collective-permute-start | bytes 1769480 | tf_op jit(solution)/shard_map/ppermute | solution.py:408
  21.3 3.9 %collective-permute-start.8 = (bf16[2,384,384]{2,1,0:T(8,128)(2,1)S(1)}, bf16[2,384,384]{2,1,0:T(8,128)(2,1)S(1)}, u32[]{:S(2)}, u32[]{:S(2)}) collective-permute-start(bf16[2,384,384]{2,1,0:T(8,128)(2,1)S(1)} %shard_map.31.both), channel_id=1, source_target_pairs={{0,1},{1,0},{2,3},{3,2},{4,5},{5,4},{6,7},{7,6},{8,9},{9,8},{10,11... | collective-permute-start | bytes 1769480 | tf_op jit(solution)/shard_map/ppermute | solution.py:412
  22.2 3.8 %collective-permute-start.1 = (bf16[2,384,384]{2,1,0:T(8,128)(2,1)S(1)}, bf16[2,384,384]{2,1,0:T(8,128)(2,1)S(1)}, u32[]{:S(2)}, u32[]{:S(2)}) collective-permute-start(bf16[2,384,384]{2,1,0:T(8,128)(2,1)S(1)} %bitcast.8), channel_id=1, source_target_pairs={{8,22},{9,23},{22,8},{23,9}} | collective-permute-start | bytes 1769480 | tf_op jit(solution)/shard_map/ppermute | solution.py:408
  22.9 3.8 %collective-permute-start.13 = (bf16[2,384,384]{2,1,0:T(8,128)(2,1)S(1)}, bf16[2,384,384]{2,1,0:T(8,128)(2,1)S(1)}, u32[]{:S(2)}, u32[]{:S(2)}) collective-permute-start(bf16[2,384,384]{2,1,0:T(8,128)(2,1)S(1)} %get-tuple-element.15.own), channel_id=1, source_target_pairs={{0,1},{1,0},{2,3},{3,2},{4,5},{5,4},{6,7},{7,6},{8,9},{9,8},{10,11... | collective-permute-start | bytes 1769480 | tf_op jit(solution)/shard_map/ppermute | solution.py:412
  23.8 21.1 %collective-permute-start.12 = (bf16[2,384,384]{2,1,0:T(8,128)(2,1)S(1)}, bf16[2,384,384]{2,1,0:T(8,128)(2,1)S(1)}, u32[]{:S(2)}, u32[]{:S(2)}) collective-permute-start(bf16[2,384,384]{2,1,0:T(8,128)(2,1)S(1)} %shard_map.32), channel_id=1, source_target_pairs={{15,29},{17,31}} | collective-permute-start | bytes 1769480 | tf_op jit(solution)/shard_map/ppermute | solution.py:408
  24.5 20.4 %collective-permute-start.11 = (bf16[2,384,384]{2,1,0:T(8,128)(2,1)S(1)}, bf16[2,384,384]{2,1,0:T(8,128)(2,1)S(1)}, u32[]{:S(2)}, u32[]{:S(2)}) collective-permute-start(bf16[2,384,384]{2,1,0:T(8,128)(2,1)S(1)} %shard_map.32), channel_id=1, source_target_pairs={{15,1},{17,3}} | collective-permute-start | bytes 1769480 | tf_op jit(solution)/shard_map/ppermute | solution.py:408
  25.2 19.7 %collective-permute-start.7 = (bf16[2,384,384]{2,1,0:T(8,128)(2,1)S(1)}, bf16[2,384,384]{2,1,0:T(8,128)(2,1)S(1)}, u32[]{:S(2)}, u32[]{:S(2)}) collective-permute-start(bf16[2,384,384]{2,1,0:T(8,128)(2,1)S(1)} %shard_map.32), channel_id=1, source_target_pairs={{22,20},{23,21},{20,6},{21,7},{10,24},{11,25},{8,10},{9,11},{12,26... | collective-permute-start | bytes 1769480 | tf_op jit(solution)/shard_map/ppermute | solution.py:408
  26.0 2.1 %collective-permute-start.10 = (bf16[2,256,384]{2,1,0:T(8,128)(2,1)S(1)}, bf16[2,256,384]{2,1,0:T(8,128)(2,1)S(1)}, u32[]{:S(2)}, u32[]{:S(2)}) collective-permute-start(bf16[2,256,384]{2,1,0:T(8,128)(2,1)S(1)} %get-tuple-element.19), channel_id=1, source_target_pairs={{14,28},{16,30}} | collective-permute-start | bytes 1179656 | tf_op jit(solution)/shard_map/ppermute | solution.py:408
  26.7 18.3 %collective-permute-start.9 = (bf16[2,256,384]{2,1,0:T(8,128)(2,1)S(1)}, bf16[2,256,384]{2,1,0:T(8,128)(2,1)S(1)}, u32[]{:S(2)}, u32[]{:S(2)}) collective-permute-start(bf16[2,256,384]{2,1,0:T(8,128)(2,1)S(1)} %get-tuple-element.19), channel_id=1, source_target_pairs={{14,0},{16,2}} | collective-permute-start | bytes 1179656 | tf_op jit(solution)/shard_map/ppermute | solution.py:408
  28.1 18.6 %collective-permute-start.16 = (bf16[2,128,384]{2,1,0:T(8,128)(2,1)S(1)}, bf16[2,128,384]{2,1,0:T(8,128)(2,1)S(1)}, u32[]{:S(2)}, u32[]{:S(2)}) collective-permute-start(bf16[2,128,384]{2,1,0:T(8,128)(2,1)S(1)} %get-tuple-element.23), channel_id=1, source_target_pairs={{14,28},{16,30}} | collective-permute-start | bytes 589832 | tf_op jit(solution)/shard_map/ppermute | solution.py:408
  45.2 9.6 %collective-permute-start.14 = (bf16[2,256,384]{2,1,0:T(8,128)(2,1)S(1)}, bf16[2,256,384]{2,1,0:T(8,128)(2,1)S(1)}, u32[]{:S(2)}, u32[]{:S(2)}) collective-permute-start(bf16[2,256,384]{2,1,0:T(8,128)(2,1)S(1)} %get-tuple-element.20.mine), channel_id=1, source_target_pairs={{0,1},{1,0},{2,3},{3,2},{4,5},{5,4},{6,7},{7,6},{8,9},{9,8},{10,11... | collective-permute-start | bytes 1179656 | tf_op jit(solution)/shard_map/ppermute | solution.py:412
  45.3 9.4 %collective-permute-start.15 = (bf16[2,128,384]{2,1,0:T(8,128)(2,1)S(1)}, bf16[2,128,384]{2,1,0:T(8,128)(2,1)S(1)}, u32[]{:S(2)}, u32[]{:S(2)}) collective-permute-start(bf16[2,128,384]{2,1,0:T(8,128)(2,1)S(1)} %get-tuple-element.23), channel_id=1, source_target_pairs={{14,0},{16,2}} | collective-permute-start | bytes 589832 | tf_op jit(solution)/shard_map/ppermute | solution.py:408
  54.7 1.7 %collective-permute-start.17 = (bf16[2,128,384]{2,1,0:T(8,128)(2,1)S(1)}, bf16[2,128,384]{2,1,0:T(8,128)(2,1)S(1)}, u32[]{:S(2)}, u32[]{:S(2)}) collective-permute-start(bf16[2,128,384]{2,1,0:T(8,128)(2,1)S(1)} %shard_map.38.tail), channel_id=1, source_target_pairs={{0,1},{1,0},{2,3},{3,2},{4,5},{5,4},{6,7},{7,6},{8,9},{9,8},{10,11... | collective-permute-start | bytes 589832 | tf_op jit(solution)/shard_map/ppermute | solution.py:412
